TPU v7x, 256 devices: a whole 4x4x8 slice. The times are simulated.
256 devices in a mesh: row: 16 (over x, y_lo, core), col: 16 (over y_hi, z).
Axes of the slice: x: 4, y: 4 (y_hi: 2, y_lo: 2; y = y_hi * 2 + y_lo), z: 8, core: 2. Of those that a mesh axis runs over, the one named last changes fastest.
Arguments:
- x_dosage: bfloat16 [32768, 4096], P('row', 'col'), may hold values from 0 to 2
- y_dosage: bfloat16 [4096, 32768], P('row', 'col'), may hold values from 0 to 2
- freq: float32 [4096], replicated, may hold values from 0.05 to 0.5
- weight: float32 [4096], replicated, may hold values from 0.5 to 3.47
- sex_rows: int32 [32768], P('row'), may hold values 0 or 1
- sex_cols: int32 [32768], P('col'), may hold values 0 or 1
Outputs:
- relation: bfloat16 [32768, 32768], P('row', 'col')
- inbreeding: float32 [32768], P('row')
All inputs are finite; a program needn't handle non-finite values. No bound on the sum of `sex_rows` or of `sex_cols` on one device may be relied on, other than what follows from the above.
Results may differ from a plain program's by a relative error of at most 0.0057.
Values may be sent and summed in bfloat16 or wider, within the bound.
A program may use at most 128 MiB of HBM per device.

v0:
```python
import jax
import jax.numpy as jnp
from jax import lax
from jax.sharding import PartitionSpec as P

STEPS = 4


def broadcast(value, axis, source):
    kept = jnp.where(lax.axis_index(axis) == source, value, 0).astype(value.dtype)
    return lax.psum(kept, axis)


def passed_along(block, axis, distance):
    devices = range(lax.axis_size(axis))
    route = [((i - distance) % len(devices), i) for i in devices]
    return lax.ppermute(block, axis, route)


def standardize(dosage, freq, weight, male):
    value = dosage.astype(jnp.float32)
    female_z = weight * (value - 2.0 * freq) / jnp.sqrt(2.0 * freq * (1.0 - freq))
    male_z = weight * (0.5 * value - freq) / jnp.sqrt(freq * (1.0 - freq))
    return jnp.where(male > 0, male_z, female_z).astype(jnp.bfloat16)


def local(x_dosage, y_dosage, freq, weight, sex_rows, sex_cols):
    group_size = y_dosage.shape[0]
    local_vars = x_dosage.shape[1]
    groups_here = local_vars // group_size
    total_vars = freq.shape[0]
    cycle_size = lax.axis_size("row")
    row_place = lax.axis_index("row")
    col_place = lax.axis_index("col")
    x_freq = lax.dynamic_slice_in_dim(freq, col_place * local_vars, local_vars)
    x_weight = lax.dynamic_slice_in_dim(weight, col_place * local_vars, local_vars)
    zx = standardize(x_dosage, x_freq[None, :], x_weight[None, :], sex_rows[:, None])
    y_freq = lax.dynamic_slice_in_dim(freq, row_place * group_size, group_size)
    y_weight = lax.dynamic_slice_in_dim(weight, row_place * group_size, group_size)
    zy = standardize(y_dosage, y_freq[:, None], y_weight[:, None], sex_cols[None, :])
    squares = jnp.sum(jnp.square(zx.astype(jnp.float32)), axis=1)
    squares = lax.psum(squares, "col")
    inbreeding = squares / jnp.float32(total_vars) - 1.0
    total = jnp.zeros((zx.shape[0], zy.shape[1]), jnp.float32)
    current = zy
    for step in range(STEPS):
        group = (row_place + step) % cycle_size
        owner = group // groups_here
        received = broadcast(zx, "col", owner)
        if step > 0:
            current = passed_along(current, "row", -1)
        total = total + jnp.dot(received, current, preferred_element_type=jnp.float32)
    relation = (total / jnp.sqrt(jnp.float32(STEPS * group_size))).astype(jnp.bfloat16)
    return (relation, inbreeding)


def solution(mesh):
    return jax.shard_map(
        local,
        mesh=mesh,
        in_specs=(P("row", "col"), P("row", "col"), P(), P(), P("row"), P("col")),
        out_specs=(P("row", "col"), P("row")),
        check_vma=False,
    )
```

profile of v0, /device:TPU:10, one launch (start us, length us, event | category | flops | bytes accessed | tf_op | source)
XLA Modules:
  0.0 256.8 jit_solution(10338738950187687271)
XLA Ops:
  7.2 0.0 all-reduce.3.cloned.1.call-start
  7.3 0.7 broadcast_compare_fusion.1
  8.0 0.8 fusion.16
  8.8 2.2 multiply_reduce_fusion
  11.0 2.1 broadcast_select_fusion
  13.1 0.0 copy-start.4
  13.1 0.0 copy-start.2
  13.1 0.0 all-reduce.3.cloned.1.call-update
  13.1 0.7 copy-done.4
  13.8 0.5 copy-done.2
  14.3 0.8 fusion.13
  15.1 0.1 collective-permute-start
  15.2 12.3 %collective-permute-done = bf16[256,2048]{1,0:T(8,128)(2,1)S(1)} collective-permute-done((bf16[256,2048]{1,0:T(8,128)(2,1)S(1)}, bf16[256,2048]{1,0:T(8,128)(2,1)S(1)}, u32[]{:S(2)}, u32[]{:S(2)}) %collective-permute-start) | collective-permute-done | bytes 1048608 | tf_op jit(solution)/shard_map/ppermute | solution.py:17
  27.5 1.9 collective-permute-start.1
  29.5 51.8 %psum.39 = f32[2048]{0:T(1024)S(1)} all-reduce(f32[2048]{0:T(1024)S(1)} %get-tuple-element.6), channel_id=1, replica_groups=mesh['row'=16,'col'=16] {'col'}, use_global_device_ids=true, to_apply=%region_5.6 | all-reduce | flops 2048 | bytes 16384 | tf_op jit(solution)/shard_map/psum | solution.py:42
  81.3 0.6 multiply_add_fusion
  81.9 0.0 collective-permute-done.1
  81.9 0.0 collective-permute-start.2
  81.9 121.8 %all-reduce.3.cloned.1.call-done = (bf16[2048,256]{1,0:T(8,128)(2,1)}, bf16[2048,256]{1,0:T(8,128)(2,1)}, bf16[2048,256]{1,0:T(8,128)(2,1)}, bf16[2048,256]{1,0:T(8,128)(2,1)}) async-done(((bf16[2048,256]{1,0:T(8,128)(2,1)}, bf16[2048,256]{1,0:T(8,128)(2,1)}, bf16[2048,256]{1,0:T(8,128)(2,1)}, bf16[2048,256]{1,0:T(8,128)(2,1)}), (bf16[2048,256]{1,0:T(8,128)(2,1)}, bf16[2048,256]{1,0:T(8,128)(2,1)}, ...) | async-done | bytes 4194320 | tf_op jit(solution)/shard_map/psum | solution.py:11
  203.7 0.0 copy-start.1
  203.7 9.4 %fusion.20 = f32[2048,2048]{1,0:T(8,128)} fusion(bf16[2048,256]{1,0:T(8,128)(2,1)} %get-tuple-element.3, bf16[256,2048]{1,0:T(8,128)(2,1)S(1)} %fusion.13), kind=kOutput, calls=%fused_computation.38 | convolution fusion | flops 2147483648 | bytes 18874368 | tf_op jit(solution)/shard_map/dot_general | solution.py:52
  213.1 0.0 copy-done.1
  213.1 0.0 copy-start
  213.1 8.1 %fusion.22 = f32[2048,2048]{1,0:T(8,128)} fusion(bf16[2048,256]{1,0:T(8,128)(2,1)S(1)} %copy-done.1, bf16[256,2048]{1,0:T(8,128)(2,1)S(1)} %collective-permute-done.1), kind=kOutput, calls=%fused_computation.40 | convolution fusion | flops 2147483648 | bytes 18874368 | tf_op jit(solution)/shard_map/dot_general | solution.py:52
  221.2 0.0 copy-done
  221.2 0.0 copy-start.3
  221.2 8.1 %fusion.21 = f32[2048,2048]{1,0:T(8,128)} fusion(bf16[2048,256]{1,0:T(8,128)(2,1)S(1)} %copy-done, bf16[256,2048]{1,0:T(8,128)(2,1)S(1)} %collective-permute-done), kind=kOutput, calls=%fused_computation.39 | convolution fusion | flops 2147483648 | bytes 18874368 | tf_op jit(solution)/shard_map/dot_general | solution.py:52
  229.3 0.0 collective-permute-done.2
  229.3 0.0 copy-done.3
  229.3 20.6 %multiply_convert_fusion = bf16[2048,2048]{1,0:T(8,128)(2,1)} fusion(f32[2048,2048]{1,0:T(8,128)} %fusion.22, f32[2048,2048]{1,0:T(8,128)} %fusion.20, f32[2048,2048]{1,0:T(8,128)} %fusion.21, bf16[2048,256]{1,0:T(8,128)(2,1)S(1)} %copy-done.3, bf16[256,2048]{1,0:T(8,128)(2,1)} %collective-permute-done.2), kind=kOutput, calls=%fused_computation | convolution fusion | flops 2168455168 | bytes 60817408 | tf_op jit(solution)/shard_map/dot_general | solution.py:52
  (3 shorter events, 0.0 us)
Async XLA Ops:
  7.2 196.6 %all-reduce.3.cloned.1.call-start = ((), (), s32[]{:S(2)}) async-start(), calls=%async_computation | async-start | bytes 8388608 | tf_op jit(solution)/shard_map/psum | solution.py:11
  13.1 0.7 copy-start.4
  13.1 1.2 copy-start.2
  15.1 12.4 %collective-permute-start = (bf16[256,2048]{1,0:T(8,128)(2,1)S(1)}, bf16[256,2048]{1,0:T(8,128)(2,1)S(1)}, u32[]{:S(2)}, u32[]{:S(2)}) collective-permute-start(bf16[256,2048]{1,0:T(8,128)(2,1)S(1)} %fusion.13), channel_id=1, source_target_pairs={{16,0},{32,16},{48,32},{64,48},{80,64},{96,80},{112,96},{128,112},... | collective-permute-start | bytes 3145736 | tf_op jit(solution)/shard_map/ppermute | solution.py:17
  27.5 54.4 %collective-permute-start.1 = (bf16[256,2048]{1,0:T(8,128)(2,1)S(1)}, bf16[256,2048]{1,0:T(8,128)(2,1)S(1)}, u32[]{:S(2)}, u32[]{:S(2)}) collective-permute-start(bf16[256,2048]{1,0:T(8,128)(2,1)S(1)} %collective-permute-done), channel_id=1, source_target_pairs={{16,0},{32,16},{48,32},{64,48},{80,64},{96,80},{112,96},{128,112},... | collective-permute-start | bytes 3145736 | tf_op jit(solution)/shard_map/ppermute | solution.py:17
  81.9 147.4 %collective-permute-start.2 = (bf16[256,2048]{1,0:T(8,128)(2,1)S(1)}, bf16[256,2048]{1,0:T(8,128)(2,1)}, u32[]{:S(2)}, u32[]{:S(2)}) collective-permute-start(bf16[256,2048]{1,0:T(8,128)(2,1)S(1)} %collective-permute-done.1), channel_id=1, source_target_pairs={{16,0},{32,16},{48,32},{64,48},{80,64},{96,80},{112,96},{128,112},... | collective-permute-start | bytes 3145736 | tf_op jit(solution)/shard_map/ppermute | solution.py:17
  203.7 9.4 %copy-start.1 = (bf16[2048,256]{1,0:T(8,128)(2,1)S(1)}, bf16[2048,256]{1,0:T(8,128)(2,1)}, u32[]{:S(2)}) copy-start(bf16[2048,256]{1,0:T(8,128)(2,1)} %get-tuple-element.2) | copy-start | bytes 3145732
  213.1 8.1 %copy-start = (bf16[2048,256]{1,0:T(8,128)(2,1)S(1)}, bf16[2048,256]{1,0:T(8,128)(2,1)}, u32[]{:S(2)}) copy-start(bf16[2048,256]{1,0:T(8,128)(2,1)} %get-tuple-element.4) | copy-start | bytes 3145732
  221.2 8.1 %copy-start.3 = (bf16[2048,256]{1,0:T(8,128)(2,1)S(1)}, bf16[2048,256]{1,0:T(8,128)(2,1)}, u32[]{:S(2)}) copy-start(bf16[2048,256]{1,0:T(8,128)(2,1)} %get-tuple-element.5) | copy-start | bytes 3145732
Sparse Core Ops, SparseCore 0:
  13.2 190.4 all-reduce.2
where the time goes:
time: 258 us; the launch traced here: 257 us
  waiting for transfers between devices  134 us (52%)
  blocking collectives  51.8 us (20%)
  matrix products  46.2 us (18%)
  between operations  14.1 us (5%)
  other arithmetic  7.23 us (3%)
    psum x1, waiting for transfers between devices, broadcast(): return lax.psum(kept, axis)  122 us
    psum x1, blocking collectives, local(): squares = lax.psum(squares, 'col')  51.8 us
    dot_general x4, matrix products, local(): jnp.dot(received, current, preferred_element_type=jnp.float32)  46.2 us
    ppermute x3, waiting for transfers between devices, passed_along(): return lax.ppermute(block, axis, route)  12.3 us
  transfers between devices with their start and end apart: 4, of which 2 were waited for; matrix products, arithmetic and copies ran while one was open for 11% of the time, Pallas kernels for 0%

commit v1 on v0

v1 whole, which is shorter than its diff:
```python
import functools

import jax
import jax.numpy as jnp
from jax import lax
from jax.experimental import pallas as pl
from jax.experimental.pallas import tpu as pltpu
from jax.sharding import PartitionSpec as P

STEPS = 4
RING = 8
CHUNKS = 16
GROUP = 256
TILE = 256
COMPUTE_ROUND = 15
PER_ROUND = 6
MESH = pl.DeviceIdType.MESH
HALF = 0.7071067811865476


def kernel(
    x_ref, y_ref, freq_arg, weight_arg, sexr_arg, sexc_arg,
    out_ref, inb_ref,
    freq_ref, weight_ref, sexr_ref, sexc_ref, xg, yg, zy, xo, pcol, acol, scol, corr, qz, qs, qp,
    send, recv, esend, ysend, yrecv, qsend, qrecv, lsem,
):
    rows, vg = x_ref.shape
    cols = y_ref.shape[1]
    half = rows // 2
    chunk = half // CHUNKS
    lanes = 128
    n_row, n_col = lax.axis_size("row"), lax.axis_size("col")
    total_vars = freq_ref.shape[0] * lanes
    r, c = lax.axis_index("row"), lax.axis_index("col")
    h, z, core = c // RING, lax.rem(c, RING), lax.rem(r, 2)
    d = lax.rem(z + 2 * RING - lax.rem(r, RING), RING)
    true = (d < STEPS) & (lax.rem(r + d, n_col) == c)
    up = {"row": r, "col": h * RING + lax.rem(z + 1, RING)}
    down = {"row": r, "col": h * RING + lax.rem(z + RING - 1, RING)}
    across = {"row": r, "col": (1 - h) * RING + z}
    mate = {"row": r + 1 - 2 * core, "col": c}
    row_m2 = {"row": lax.rem(r + n_row - 2, n_row), "col": c}
    row_p2 = {"row": lax.rem(r + 2, n_row), "col": c}
    row_m3 = {"row": lax.rem(r + n_row - 3, n_row), "col": c}
    row_3 = {"row": lax.rem(r + n_row - 3 + 6 * core, n_row), "col": c}
    way = (up, down)

    barrier = pltpu.get_barrier_semaphore()
    friends = (up, down, across, mate, row_m2, row_p2, row_3)
    for friend in friends:
        pl.semaphore_signal(barrier, inc=1, device_id=friend, device_id_type=MESH)

    own_cols = pl.ds(pl.multiple_of(lax.rem(d, STEPS) * vg, vg), vg)
    local_xo = pltpu.make_async_copy(x_ref, xo, lsem.at[0])
    local_y = pltpu.make_async_copy(y_ref, yg.at[pl.ds(0, vg)], lsem.at[1])
    local_xg = pltpu.make_async_copy(x_ref, xg.at[:, own_cols], lsem.at[2])
    small = [
        pltpu.make_async_copy(arg, to, lsem.at[3 + at])
        for at, (arg, to) in enumerate(
            ((freq_arg, freq_ref), (weight_arg, weight_ref), (sexr_arg, sexr_ref), (sexc_arg, sexc_ref))
        )
    ]
    local_xo.start()
    local_y.start()
    for copy in small:
        copy.start()

    @pl.when(true)
    def _():
        local_xg.start()

    pl.semaphore_wait(barrier, len(friends))

    def order(side, i):
        if side == 0:
            s = lax.rem(jnp.minimum(d, STEPS - 1) + STEPS - i, STEPS)
            n = lax.rem(d - s + RING, RING)
        else:
            s = lax.rem(jnp.where(d < STEPS, d, 0) + i, STEPS)
            n = lax.rem(s - d + RING, RING)
        return s, n

    def x_copy(side, s, j, from_arg=False, to_across=False):
        at = pl.ds(pl.multiple_of(side * half + j * chunk, chunk), chunk)
        place = xg.at[at, pl.ds(pl.multiple_of(s * vg, vg), vg)]
        return pltpu.make_async_remote_copy(
            src_ref=x_ref.at[at] if from_arg else place,
            dst_ref=place,
            send_sem=esend.at[side, j] if to_across else send.at[side, s, j],
            recv_sem=recv.at[side, s, j],
            device_id=across if to_across else way[side],
            device_id_type=MESH,
        )

    def y_copy(slot_from, slot_to, sem, target, from_arg=False):
        return pltpu.make_async_remote_copy(
            src_ref=y_ref if from_arg else yg.at[pl.ds(slot_from * vg, vg)],
            dst_ref=yg.at[pl.ds(slot_to * vg, vg)],
            send_sem=ysend.at[sem],
            recv_sem=yrecv.at[slot_to],
            device_id=target,
            device_id_type=MESH,
        )

    y_mate = y_copy(0, 1, 0, mate, True)
    y_two = y_copy(0, 2, 1, row_m2, True)
    y_three = y_copy(0, 3, 2, row_m3, True)
    y_relay1 = y_copy(2, 1, 3, mate)
    y_relay3 = y_copy(2, 3, 3, mate)

    def spread(vector):
        return jnp.broadcast_to(vector, (lanes, lanes)).T

    def tables():
        for copy in small:
            copy.wait()
        for s in range(STEPS):
            for part in range(vg // lanes):
                at = lax.rem(r + s, n_row) * (vg // lanes) + part
                f, w = freq_ref[pl.ds(at, 1), :], weight_ref[pl.ds(at, 1), :]
                to = pl.ds(s * vg + part * lanes, lanes)
                pcol[to, :] = spread(2.0 * f)
                acol[to, :] = spread(w * w / (2.0 * f * (1.0 - f)) / jnp.sqrt(jnp.float32(STEPS * vg)))
        for g in range(rows // lanes):
            scale = jnp.where(sexr_ref[pl.ds(g, 1), :] > 0, HALF, 1.0).astype(jnp.float32)
            scol[pl.ds(g * lanes, lanes), :] = spread(scale)

    def squares():
        local_xo.wait()
        parts = vg // lanes
        ps, scales = [], []
        for part in range(parts):
            at = c * parts + part
            f, w = freq_ref[pl.ds(at, 1), :], weight_ref[pl.ds(at, 1), :]
            ps.append(2.0 * f)
            scales.append(w / jnp.sqrt(2.0 * f * (1.0 - f)))

        @pl.loop(0, rows // lanes)
        def _(g):
            block = xo[pl.ds(pl.multiple_of(g * lanes, lanes), lanes), :].astype(jnp.float32)
            summed = jnp.zeros((lanes, lanes), jnp.float32)
            for part in range(parts):
                value = (block[:, part * lanes:(part + 1) * lanes] - ps[part]) * scales[part]
                summed = summed + value * value
            line = jnp.sum(summed.T, axis=0, keepdims=True)
            line = jnp.where(sexr_ref[pl.ds(g, 1), :] > 0, 0.5 * line, line)
            qz[z, pl.ds(g, 1), :] = line

    def q_copy(side, step):
        shift = step if side else RING - step
        at = lax.rem(z + shift, RING)
        return pltpu.make_async_remote_copy(
            src_ref=qz.at[at], dst_ref=qz.at[at],
            send_sem=qsend.at[side, step], recv_sem=qrecv.at[side, step],
            device_id=way[side], device_id_type=MESH,
        )

    def q_wait(side, step):
        shift = step if side else RING - step
        at = lax.rem(z + shift, RING)
        pltpu.make_async_remote_copy(
            src_ref=qz.at[at], dst_ref=qz.at[at],
            send_sem=qsend.at[side, step], recv_sem=qrecv.at[side, step - 1],
            device_id=way[side], device_id_type=MESH,
        ).wait_recv()

    far = (RING // 2, RING // 2 - 1)

    def q_start():
        for side in range(2):
            q_copy(side, 0).start()

    def q_step(step):
        for side in range(2):
            if step <= far[side]:
                q_wait(side, step)
                if step < far[side]:
                    q_copy(side, step).start()

    q_across = pltpu.make_async_remote_copy(
        src_ref=qs, dst_ref=qp, send_sem=qsend.at[0, 7], recv_sem=qrecv.at[0, 7],
        device_id=across, device_id_type=MESH,
    )

    def q_sum():
        summed = qz[0]
        for at in range(1, RING):
            summed = summed + qz[at]
        qs[...] = summed

    def q_end():
        q_across.wait_recv()
        inb_ref[...] = (qs[...] + qp[...]) / jnp.float32(total_vars) - 1.0

    def transform(slot):
        @pl.loop(0, cols // lanes)
        def _(g):
            at, to = pl.ds(slot * vg, vg), pl.ds(pl.multiple_of(g * lanes, lanes), lanes)
            scale = jnp.where(sexc_ref[pl.ds(g, 1), :] > 0, HALF, 1.0).astype(jnp.float32)
            p = pcol[at, :]
            value = (yg[at, to].astype(jnp.float32) - p) * acol[at, :] * scale
            rounded = value.astype(jnp.bfloat16)
            zy[at, to] = rounded
            sums = jnp.sum(rounded.astype(jnp.float32) * p, axis=0, keepdims=True)
            corr[:, to] = sums if slot == 0 else corr[:, to] + sums

    def piece(side, q, t):
        at = pl.ds(pl.multiple_of(side * half + q * GROUP, GROUP), GROUP)
        to = pl.ds(pl.multiple_of(t * TILE, TILE), TILE)
        total = jnp.dot(xg[at, :], zy[:, to], preferred_element_type=jnp.float32)
        scale = jnp.concatenate([scol[at, :]] * (TILE // lanes), axis=1)
        out_ref[at, to] = ((total - corr[:, to]) * scale).astype(out_ref.dtype)

    def y_first():
        local_y.wait()
        transform(0)

    def y_sends():
        y_two.start()

        @pl.when(core == 0)
        def _():
            y_three.start()

        @pl.when(core == 1)
        def _():
            y_mate.start()

    def y_second():
        y_two.wait_recv()

        @pl.when(core == 0)
        def _():
            y_relay1.start()

        @pl.when(core == 1)
        def _():
            y_relay3.start()

        transform(2)

    def y_near():
        y_mate.wait_recv()
        transform(1)

    def x_own():
        @pl.when(true)
        def _():
            local_xg.wait()

    def y_far():
        y_three.wait_recv()
        transform(3)

    tasks = {
        0: (y_sends, tables), 1: (y_first,), 2: (squares,), 4: (q_start,), 5: (lambda: q_step(1),),
        6: (lambda: q_step(2),), 8: (lambda: q_step(3),), 9: (lambda: q_step(4), q_sum),
        11: (q_across.start,), 12: (y_second,), 13: (y_near,), 14: (y_far, q_end, x_own),
    }

    tiles = cols // TILE
    groups = half // GROUP

    @pl.loop(0, CHUNKS + RING - 1)
    def _(now):
        for side in range(2):
            for i in range(STEPS):
                s, n = order(side, i)
                j = now - n

                @pl.when((j >= 0) & (j < CHUNKS))
                def _():
                    mine = (n == 0) & true

                    @pl.when(mine)
                    def _():
                        x_copy(side, s, j, True).start()
                        x_copy(side, s, j, True, True).start()

                    @pl.when(jnp.logical_not(mine))
                    def _():
                        hop = x_copy(side, s, j)
                        hop.wait_recv()

                        @pl.when(n < RING - 1)
                        def _():
                            hop.start()

        for at, jobs in tasks.items():
            @pl.when(now == at)
            def _():
                for job in jobs:
                    job()

        @pl.when(now >= COMPUTE_ROUND)
        def _():
            @pl.loop(0, PER_ROUND)
            def _(k):
                number = (now - COMPUTE_ROUND) * PER_ROUND + k
                piece(lax.rem(number, 2 * tiles) // tiles, number // (2 * tiles), lax.rem(number, tiles))

    @pl.loop(0, 2 * tiles)
    def _(k):
        piece(k // tiles, groups - 1, lax.rem(k, tiles))

    @pl.loop(0, CHUNKS)
    def _(j):
        for side in range(2):
            for i in range(STEPS):
                s, n = order(side, i)

                @pl.when(n < RING - 1)
                def _():
                    x_copy(side, s, j).wait_send()

            @pl.when(true)
            def _():
                x_copy(side, lax.rem(d, STEPS), j, False, True).wait_send()

    for side in range(2):
        for step in range(far[side]):
            q_copy(side, step).wait_send()
    q_across.wait_send()
    y_two.wait_send()
    y_relay1.wait_send()

    @pl.when(core == 0)
    def _():
        y_three.wait_send()

    @pl.when(core == 1)
    def _():
        y_mate.wait_send()


def local(x_dosage, y_dosage, freq, weight, sex_rows, sex_cols):
    rows, vg = x_dosage.shape
    cols = y_dosage.shape[1]
    lanes = 128
    groups = rows // lanes
    vmem = pl.BlockSpec(memory_space=pltpu.VMEM)
    hbm = pl.BlockSpec(memory_space=pltpu.HBM)
    relation, inbreeding = pl.pallas_call(
        kernel,
        out_shape=(
            pltpu.VMEM((rows, cols), jnp.bfloat16),
            pltpu.VMEM((groups, lanes), jnp.float32),
        ),
        in_specs=[hbm] * 6,
        out_specs=(vmem, vmem),
        scratch_shapes=[
            pltpu.VMEM((freq.shape[0] // lanes, lanes), jnp.float32),
            pltpu.VMEM((freq.shape[0] // lanes, lanes), jnp.float32),
            pltpu.VMEM((groups, lanes), jnp.int32),
            pltpu.VMEM((cols // lanes, lanes), jnp.int32),
            pltpu.VMEM((rows, STEPS * vg), jnp.bfloat16),
            pltpu.VMEM((STEPS * vg, cols), jnp.bfloat16),
            pltpu.VMEM((STEPS * vg, cols), jnp.bfloat16),
            pltpu.VMEM((rows, vg), jnp.bfloat16),
            pltpu.VMEM((STEPS * vg, lanes), jnp.float32),
            pltpu.VMEM((STEPS * vg, lanes), jnp.float32),
            pltpu.VMEM((rows, lanes), jnp.float32),
            pltpu.VMEM((1, cols), jnp.float32),
            pltpu.VMEM((RING, groups, lanes), jnp.float32),
            pltpu.VMEM((groups, lanes), jnp.float32),
            pltpu.VMEM((groups, lanes), jnp.float32),
            pltpu.SemaphoreType.DMA((2, STEPS, CHUNKS)),
            pltpu.SemaphoreType.DMA((2, STEPS, CHUNKS)),
            pltpu.SemaphoreType.DMA((2, CHUNKS)),
            pltpu.SemaphoreType.DMA((4,)),
            pltpu.SemaphoreType.DMA((4,)),
            pltpu.SemaphoreType.DMA((2, 8)),
            pltpu.SemaphoreType.DMA((2, 8)),
            pltpu.SemaphoreType.DMA((7,)),
        ],
        compiler_params=pltpu.CompilerParams(
            collective_id=0, has_side_effects=True, vmem_limit_bytes=48 * 1024 * 1024
        ),
        name="window",
    )(
        x_dosage, y_dosage, freq.reshape(-1, lanes), weight.reshape(-1, lanes),
        sex_rows.reshape(-1, lanes), sex_cols.reshape(-1, lanes),
    )
    return relation, inbreeding.reshape(rows)


def solution(mesh):
    return jax.shard_map(
        local,
        mesh=mesh,
        in_specs=(P("row", "col"), P("row", "col"), P(), P(), P("row"), P("col")),
        out_specs=(P("row", "col"), P("row")),
        check_vma=False,
    )
```

time: 258 us -> 150 us (0.58)
  Pallas kernels: 0 us -> 145 us
  waiting for transfers between devices: 134 us -> 0 us
  blocking collectives: 51.8 us -> 0 us
  matrix products: 46.2 us -> 0 us
  between operations: 14.1 us -> 0.64 us
  other arithmetic: 7.23 us -> 0 us
  local copies, waits for them, and re-layouts: 1.21 us -> 4 us
    pallas_call x0 -> x1, Pallas kernels: none -> 145 us  [local(): pl.pallas_call(kernel, out_shape=(pltpu.VMEM((rows, cols), jnp.bfloat16),...]
    psum x1 -> x0, waiting for transfers between devices: 122 us -> none  [broadcast(): return lax.psum(kept, axis)]
    psum x1 -> x0, blocking collectives: 51.8 us -> none  [local(): squares = lax.psum(squares, 'col')]
    dot_general x4 -> x0, matrix products: 46.2 us -> none  [local(): jnp.dot(received, current, preferred_element_type=jnp.float32)]
    ppermute x3 -> x0, waiting for transfers between devices: 12.3 us -> none  [passed_along(): return lax.ppermute(block, axis, route)]
    unnamed x10 -> x2, local copies, waits for them, and re-layouts: 1.21 us -> 4 us
  transfers between devices with their start and end apart: 4 -> 0, of which waited for: 2 -> 0; matrix products, arithmetic and copies ran while one was open for 11% -> 0% of each run, Pallas kernels for 0% -> 0%
where the time goes in v1:
time: 150 us
  Pallas kernels  145 us (97%)
  local copies, waits for them, and re-layouts  4 us (3%)
    pallas_call x1, Pallas kernels, local(): pl.pallas_call(kernel, out_shape=(pltpu.VMEM((rows, cols), jnp.bfloat16),...  145 us
    unnamed x2, local copies, waits for them, and re-layouts  4 us

profile of v1, /device:TPU:10, one launch (start us, length us, event | category | flops | bytes accessed | tf_op | source)
XLA Modules:
  0.0 149.9 jit_solution(13136375094689750929)
XLA Ops:
  0.6 145.3 %window.1 = (bf16[2048,2048]{1,0:T(8,128)(2,1)S(1)}, f32[16,128]{1,0:T(8,128)S(1)}) custom-call(bf16[2048,256]{1,0:T(8,128)(2,1)} %x_ref.1, bf16[256,2048]{1,0:T(8,128)(2,1)} %y_ref.1, f32[32,128]{1,0:T(8,128)} %bitcast.6, f32[32,128]{1,0:T(8,128)} %bitcast.7, s32[16,128]{1,0:T(8,128)} %bitcast.8, s32[16,128]{1,0:T(8,128)} %bitcast.9), custom_call_target="tpu_custom_call" | custom-call | tf_op jit(solution)/shard_map/window/pallas_call | solution.py:343
  145.9 3.4 %copy.10 = bf16[2048,2048]{1,0:T(8,128)(2,1)} copy(bf16[2048,2048]{1,0:T(8,128)(2,1)S(1)} %get-tuple-element.6) | data formatting | bytes 16777216
  149.3 0.6 copy.11

commit v2 on v1

--- a/solution.py
+++ b/solution.py
@@ -12,8 +12,10 @@
 CHUNKS = 16
 GROUP = 256
 TILE = 256
-COMPUTE_ROUND = 15
+SKEW = 2
+COMPUTE_ROUND = 21
 PER_ROUND = 6
+LATE, SECOND, NEAR, FAR = 10, 17, 19, 20
 MESH = pl.DeviceIdType.MESH
 HALF = 0.7071067811865476
 
@@ -92,6 +94,13 @@
             device_id_type=MESH,
         )
 
+    @pl.when(true)
+    def _():
+        @pl.loop(0, CHUNKS)
+        def _(j):
+            for side in range(2):
+                x_copy(side, lax.rem(d, STEPS), j, True, True).start()
+
     def y_copy(slot_from, slot_to, sem, target, from_arg=False):
         return pltpu.make_async_remote_copy(
             src_ref=y_ref if from_arg else yg.at[pl.ds(slot_from * vg, vg)],
@@ -215,8 +224,15 @@
         local_y.wait()
         transform(0)
 
+    y_low = lax.rem(r // 2, 2)
+
+    def y_two_start(low):
+        @pl.when(y_low == low)
+        def _():
+            y_two.start()
+
     def y_sends():
-        y_two.start()
+        y_two_start(1)
 
         @pl.when(core == 0)
         def _():
@@ -255,18 +271,20 @@
     tasks = {
         0: (y_sends, tables), 1: (y_first,), 2: (squares,), 4: (q_start,), 5: (lambda: q_step(1),),
         6: (lambda: q_step(2),), 8: (lambda: q_step(3),), 9: (lambda: q_step(4), q_sum),
-        11: (q_across.start,), 12: (y_second,), 13: (y_near,), 14: (y_far, q_end, x_own),
+        LATE: (lambda: y_two_start(0),), 11: (q_across.start,), 14: (q_end, x_own), SECOND: (y_second,), NEAR: (y_near,), FAR: (y_far,),
     }
 
     tiles = cols // TILE
     groups = half // GROUP
 
-    @pl.loop(0, CHUNKS + RING - 1)
+    orders = [[order(side, i) for i in range(STEPS)] for side in range(2)]
+
+    @pl.loop(0, CHUNKS + SKEW * (RING - 1))
     def _(now):
-        for side in range(2):
-            for i in range(STEPS):
-                s, n = order(side, i)
-                j = now - n
+        for i in range(STEPS):
+            for side in range(2):
+                s, n = orders[side][i]
+                j = now - SKEW * n
 
                 @pl.when((j >= 0) & (j < CHUNKS))
                 def _():
@@ -275,7 +293,6 @@
                     @pl.when(mine)
                     def _():
                         x_copy(side, s, j, True).start()
-                        x_copy(side, s, j, True, True).start()
 
                     @pl.when(jnp.logical_not(mine))
                     def _():
@@ -297,7 +314,10 @@
             @pl.loop(0, PER_ROUND)
             def _(k):
                 number = (now - COMPUTE_ROUND) * PER_ROUND + k
-                piece(lax.rem(number, 2 * tiles) // tiles, number // (2 * tiles), lax.rem(number, tiles))
+
+                @pl.when(number < 2 * tiles * (groups - 1))
+                def _():
+                    piece(lax.rem(number, 2 * tiles) // tiles, number // (2 * tiles), lax.rem(number, tiles))
 
     @pl.loop(0, 2 * tiles)
     def _(k):

time: 150 us -> 102 us (0.68)
  the two profiles are of different devices: /device:TPU:10 before, /device:TPU:6 now
where the time goes in v2:
time: 102 us
  Pallas kernels  97.3 us (95%)
  local copies, waits for them, and re-layouts  4 us (4%)
    pallas_call x1, Pallas kernels, local(): pl.pallas_call(kernel, out_shape=(pltpu.VMEM((rows, cols), jnp.bfloat16),...  97.3 us
    unnamed x2, local copies, waits for them, and re-layouts  4 us

profile of v2, /device:TPU:6, one launch (start us, length us, event | category | flops | bytes accessed | tf_op | source)
XLA Modules:
  0.0 101.9 jit_solution(7400731337145031933)
XLA Ops:
  0.6 97.3 %window.1 = (bf16[2048,2048]{1,0:T(8,128)(2,1)S(1)}, f32[16,128]{1,0:T(8,128)S(1)}) custom-call(bf16[2048,256]{1,0:T(8,128)(2,1)} %x_ref.1, bf16[256,2048]{1,0:T(8,128)(2,1)} %y_ref.1, f32[32,128]{1,0:T(8,128)} %bitcast.6, f32[32,128]{1,0:T(8,128)} %bitcast.7, s32[16,128]{1,0:T(8,128)} %bitcast.8, s32[16,128]{1,0:T(8,128)} %bitcast.9), custom_call_target="tpu_custom_call" | custom-call | tf_op jit(solution)/shard_map/window/pallas_call | solution.py:363
  97.9 3.4 %copy.10 = bf16[2048,2048]{1,0:T(8,128)(2,1)} copy(bf16[2048,2048]{1,0:T(8,128)(2,1)S(1)} %get-tuple-element.6) | data formatting | bytes 16777216
  101.3 0.6 copy.11

commit v3 on v2

--- a/solution.py
+++ b/solution.py
@@ -10,12 +10,10 @@
 STEPS = 4
 RING = 8
 CHUNKS = 16
-GROUP = 256
-TILE = 256
+TILE = 512
 SKEW = 2
-COMPUTE_ROUND = 21
-PER_ROUND = 6
-LATE, SECOND, NEAR, FAR = 10, 17, 19, 20
+LATE, SECOND, NEAR, FAR = 12, 19, 21, 21
+EDGES, MIDDLES, PER_EDGE, PER_MIDDLE = 22, 26, 2, 2
 MESH = pl.DeviceIdType.MESH
 HALF = 0.7071067811865476
 
@@ -83,7 +81,7 @@
         return s, n
 
     def x_copy(side, s, j, from_arg=False, to_across=False):
-        at = pl.ds(pl.multiple_of(side * half + j * chunk, chunk), chunk)
+        at = pl.ds(pl.multiple_of(j * chunk if side == 0 else rows - (j + 1) * chunk, chunk), chunk)
         place = xg.at[at, pl.ds(pl.multiple_of(s * vg, vg), vg)]
         return pltpu.make_async_remote_copy(
             src_ref=x_ref.at[at] if from_arg else place,
@@ -213,8 +211,8 @@
             sums = jnp.sum(rounded.astype(jnp.float32) * p, axis=0, keepdims=True)
             corr[:, to] = sums if slot == 0 else corr[:, to] + sums
 
-    def piece(side, q, t):
-        at = pl.ds(pl.multiple_of(side * half + q * GROUP, GROUP), GROUP)
+    def piece(start, size, t):
+        at = pl.ds(pl.multiple_of(start, lanes), size)
         to = pl.ds(pl.multiple_of(t * TILE, TILE), TILE)
         total = jnp.dot(xg[at, :], zy[:, to], preferred_element_type=jnp.float32)
         scale = jnp.concatenate([scol[at, :]] * (TILE // lanes), axis=1)
@@ -224,15 +222,20 @@
         local_y.wait()
         transform(0)
 
-    y_low = lax.rem(r // 2, 2)
-
-    def y_two_start(low):
-        @pl.when(y_low == low)
+    def sends_across(row):
+        far_d = lax.rem(z + 2 * RING - lax.rem(row, RING), RING)
+        return (far_d < STEPS) & (lax.rem(row + far_d, n_col) == c)
+
+    on_path = lax.rem(r - core + n_row - jnp.where(lax.rem(r // 2, 2) == 0, 4, 0), n_row)
+    crowded = sends_across(on_path) | sends_across(on_path + 1)
+
+    def y_two_start(held):
+        @pl.when(crowded if held else jnp.logical_not(crowded))
         def _():
             y_two.start()
 
     def y_sends():
-        y_two_start(1)
+        y_two_start(False)
 
         @pl.when(core == 0)
         def _():
@@ -268,14 +271,15 @@
         y_three.wait_recv()
         transform(3)
 
-    tasks = {
-        0: (y_sends, tables), 1: (y_first,), 2: (squares,), 4: (q_start,), 5: (lambda: q_step(1),),
-        6: (lambda: q_step(2),), 8: (lambda: q_step(3),), 9: (lambda: q_step(4), q_sum),
-        LATE: (lambda: y_two_start(0),), 11: (q_across.start,), 14: (q_end, x_own), SECOND: (y_second,), NEAR: (y_near,), FAR: (y_far,),
-    }
+    tasks = (
+        (0, y_sends), (3, tables), (5, y_first), (7, squares), (9, q_start), (11, lambda: q_step(1)),
+        (12, lambda: q_step(2)), (13, lambda: q_step(3)), (14, lambda: q_step(4)), (14, q_sum),
+        (16, q_across.start), (21, q_end), (21, x_own), (LATE, lambda: y_two_start(True)),
+        (SECOND, y_second), (NEAR, y_near), (FAR, y_far),
+    )
 
     tiles = cols // TILE
-    groups = half // GROUP
+    edge, middle = rows // 4, rows // 8
 
     orders = [[order(side, i) for i in range(STEPS)] for side in range(2)]
 
@@ -303,25 +307,32 @@
                         def _():
                             hop.start()
 
-        for at, jobs in tasks.items():
-            @pl.when(now == at)
-            def _():
-                for job in jobs:
-                    job()
-
-        @pl.when(now >= COMPUTE_ROUND)
-        def _():
-            @pl.loop(0, PER_ROUND)
+        for at, job in tasks:
+            pl.when(now == at)(job)
+
+        @pl.when((now >= EDGES) & (now < MIDDLES))
+        def _():
+            @pl.loop(0, PER_EDGE)
             def _(k):
-                number = (now - COMPUTE_ROUND) * PER_ROUND + k
-
-                @pl.when(number < 2 * tiles * (groups - 1))
+                number = (now - EDGES) * PER_EDGE + k
+
+                @pl.when(number < 2 * tiles)
                 def _():
-                    piece(lax.rem(number, 2 * tiles) // tiles, number // (2 * tiles), lax.rem(number, tiles))
-
-    @pl.loop(0, 2 * tiles)
-    def _(k):
-        piece(k // tiles, groups - 1, lax.rem(k, tiles))
+                    piece(number // tiles * (rows - edge), edge, lax.rem(number, tiles))
+
+        @pl.when(now >= MIDDLES)
+        def _():
+            @pl.loop(0, PER_MIDDLE)
+            def _(k):
+                number = (now - MIDDLES) * PER_MIDDLE + k
+
+                @pl.when(number < 2 * tiles)
+                def _():
+                    piece(edge + number // tiles * (rows - 2 * edge - middle), middle, lax.rem(number, tiles))
+
+    @pl.loop(0, tiles)
+    def _(t):
+        piece(edge + middle, rows - 2 * (edge + middle), t)
 
     @pl.loop(0, CHUNKS)
     def _(j):

time: 102 us -> 89.6 us (0.88)
  the two profiles are of different devices: /device:TPU:6 before, /device:TPU:10 now
where the time goes in v3:
time: 89.6 us; the launch traced here: 89.5 us
  Pallas kernels  84.8 us (95%)
  local copies, waits for them, and re-layouts  4 us (4%)
    pallas_call x1, Pallas kernels, local(): pl.pallas_call(kernel, out_shape=(pltpu.VMEM((rows, cols), jnp.bfloat16),...  84.8 us
    unnamed x2, local copies, waits for them, and re-layouts  4 us

profile of v3, /device:TPU:10, one launch (start us, length us, event | category | flops | bytes accessed | tf_op | source)
XLA Modules:
  0.0 89.5 jit_solution(16632383298333720520)
XLA Ops:
  0.6 84.8 %window.1 = (bf16[2048,2048]{1,0:T(8,128)(2,1)S(1)}, f32[16,128]{1,0:T(8,128)S(1)}) custom-call(bf16[2048,256]{1,0:T(8,128)(2,1)} %x_ref.1, bf16[256,2048]{1,0:T(8,128)(2,1)} %y_ref.1, f32[32,128]{1,0:T(8,128)} %bitcast.6, f32[32,128]{1,0:T(8,128)} %bitcast.7, s32[16,128]{1,0:T(8,128)} %bitcast.8, s32[16,128]{1,0:T(8,128)} %bitcast.9), custom_call_target="tpu_custom_call" | custom-call | tf_op jit(solution)/shard_map/window/pallas_call | solution.py:374
  85.5 3.4 %copy.10 = bf16[2048,2048]{1,0:T(8,128)(2,1)} copy(bf16[2048,2048]{1,0:T(8,128)(2,1)S(1)} %get-tuple-element.6) | data formatting | bytes 16777216
  88.9 0.6 copy.11

commit v4 on v3

--- a/solution.py
+++ b/solution.py
@@ -9,11 +9,11 @@
 
 STEPS = 4
 RING = 8
-CHUNKS = 16
+CHUNKS = 8
 TILE = 512
-SKEW = 2
-LATE, SECOND, NEAR, FAR = 12, 19, 21, 21
-EDGES, MIDDLES, PER_EDGE, PER_MIDDLE = 22, 26, 2, 2
+SKEW = 1
+LATE, EARLY, SECOND, LAST = 6, 8, 9, 10
+EDGES, MIDDLES = 11, 13
 MESH = pl.DeviceIdType.MESH
 HALF = 0.7071067811865476
 
@@ -92,17 +92,18 @@
             device_id_type=MESH,
         )
 
-    @pl.when(true)
-    def _():
-        @pl.loop(0, CHUNKS)
-        def _(j):
-            for side in range(2):
-                x_copy(side, lax.rem(d, STEPS), j, True, True).start()
+    def exchange():
+        @pl.when(true)
+        def _():
+            @pl.loop(0, CHUNKS)
+            def _(j):
+                for side in range(2):
+                    x_copy(side, lax.rem(d, STEPS), j, True, True).start()
 
     def y_copy(slot_from, slot_to, sem, target, from_arg=False):
         return pltpu.make_async_remote_copy(
             src_ref=y_ref if from_arg else yg.at[pl.ds(slot_from * vg, vg)],
-            dst_ref=yg.at[pl.ds(slot_to * vg, vg)],
+            dst_ref=yg.at[pl.ds(pl.multiple_of(slot_to * vg, vg), vg)],
             send_sem=ysend.at[sem],
             recv_sem=yrecv.at[slot_to],
             device_id=target,
@@ -199,17 +200,17 @@
         q_across.wait_recv()
         inb_ref[...] = (qs[...] + qp[...]) / jnp.float32(total_vars) - 1.0
 
-    def transform(slot):
+    def transform(slot, first=False):
         @pl.loop(0, cols // lanes)
         def _(g):
-            at, to = pl.ds(slot * vg, vg), pl.ds(pl.multiple_of(g * lanes, lanes), lanes)
+            at, to = pl.ds(pl.multiple_of(slot * vg, vg), vg), pl.ds(pl.multiple_of(g * lanes, lanes), lanes)
             scale = jnp.where(sexc_ref[pl.ds(g, 1), :] > 0, HALF, 1.0).astype(jnp.float32)
             p = pcol[at, :]
             value = (yg[at, to].astype(jnp.float32) - p) * acol[at, :] * scale
             rounded = value.astype(jnp.bfloat16)
             zy[at, to] = rounded
             sums = jnp.sum(rounded.astype(jnp.float32) * p, axis=0, keepdims=True)
-            corr[:, to] = sums if slot == 0 else corr[:, to] + sums
+            corr[:, to] = sums if first else corr[:, to] + sums
 
     def piece(start, size, t):
         at = pl.ds(pl.multiple_of(start, lanes), size)
@@ -220,7 +221,7 @@
 
     def y_first():
         local_y.wait()
-        transform(0)
+        transform(0, True)
 
     def sends_across(row):
         far_d = lax.rem(z + 2 * RING - lax.rem(row, RING), RING)
@@ -258,24 +259,24 @@
 
         transform(2)
 
-    def y_near():
-        y_mate.wait_recv()
-        transform(1)
-
     def x_own():
         @pl.when(true)
         def _():
             local_xg.wait()
 
-    def y_far():
-        y_three.wait_recv()
-        transform(3)
+    def y_early():
+        y_copy(0, 1 + 2 * core, 0, mate).wait_recv()
+        transform(1 + 2 * core)
+
+    def y_last():
+        y_copy(0, 3 - 2 * core, 0, mate).wait_recv()
+        transform(3 - 2 * core)
 
     tasks = (
-        (0, y_sends), (3, tables), (5, y_first), (7, squares), (9, q_start), (11, lambda: q_step(1)),
-        (12, lambda: q_step(2)), (13, lambda: q_step(3)), (14, lambda: q_step(4)), (14, q_sum),
-        (16, q_across.start), (21, q_end), (21, x_own), (LATE, lambda: y_two_start(True)),
-        (SECOND, y_second), (NEAR, y_near), (FAR, y_far),
+        (-1, exchange), (-1, y_sends), (1, tables), (2, y_first), (3, squares), (4, q_start), (5, lambda: q_step(1)),
+        (6, lambda: q_step(2)), (7, lambda: q_step(3)), (8, lambda: q_step(4)), (8, q_sum),
+        (9, q_across.start), (10, x_own), (LATE, lambda: y_two_start(True)),
+        (EARLY, y_early), (SECOND, y_second), (LAST, y_last), (12, q_end),
     )
 
     tiles = cols // TILE
@@ -285,6 +286,9 @@
 
     @pl.loop(0, CHUNKS + SKEW * (RING - 1))
     def _(now):
+        for at, job in tasks:
+            pl.when(now == at + 1)(job)
+
         for i in range(STEPS):
             for side in range(2):
                 s, n = orders[side][i]
@@ -307,28 +311,15 @@
                         def _():
                             hop.start()
 
-        for at, job in tasks:
-            pl.when(now == at)(job)
-
-        @pl.when((now >= EDGES) & (now < MIDDLES))
-        def _():
-            @pl.loop(0, PER_EDGE)
-            def _(k):
-                number = (now - EDGES) * PER_EDGE + k
-
-                @pl.when(number < 2 * tiles)
-                def _():
-                    piece(number // tiles * (rows - edge), edge, lax.rem(number, tiles))
-
-        @pl.when(now >= MIDDLES)
-        def _():
-            @pl.loop(0, PER_MIDDLE)
-            def _(k):
-                number = (now - MIDDLES) * PER_MIDDLE + k
-
-                @pl.when(number < 2 * tiles)
-                def _():
-                    piece(edge + number // tiles * (rows - 2 * edge - middle), middle, lax.rem(number, tiles))
+            @pl.when((now >= EDGES) & (now < MIDDLES))
+            def _():
+                number = (now - EDGES) * STEPS + i
+                piece(number // tiles * (rows - edge), edge, lax.rem(number, tiles))
+
+            @pl.when(now >= MIDDLES)
+            def _():
+                number = (now - MIDDLES) * STEPS + i
+                piece(edge + number // tiles * (rows - 2 * edge - middle), middle, lax.rem(number, tiles))
 
     @pl.loop(0, tiles)
     def _(t):

time: 89.6 us -> 87.5 us (0.977)
  Pallas kernels: 84.8 us -> 82.8 us
    pallas_call x1, Pallas kernels: 84.8 us -> 82.8 us  [local(): pl.pallas_call(kernel, out_shape=(pltpu.VMEM((rows, cols), jnp.bfloat16),...]
where the time goes in v4:
time: 87.5 us; the launch traced here: 87.4 us
  Pallas kernels  82.8 us (95%)
  local copies, waits for them, and re-layouts  4 us (5%)
    pallas_call x1, Pallas kernels, local(): pl.pallas_call(kernel, out_shape=(pltpu.VMEM((rows, cols), jnp.bfloat16),...  82.8 us
    unnamed x2, local copies, waits for them, and re-layouts  4 us

profile of v4, /device:TPU:10, one launch (start us, length us, event | category | flops | bytes accessed | tf_op | source)
XLA Modules:
  0.0 87.4 jit_solution(1402456516259948465)
XLA Ops:
  0.6 82.8 %window.1 = (bf16[2048,2048]{1,0:T(8,128)(2,1)S(1)}, f32[16,128]{1,0:T(8,128)S(1)}) custom-call(bf16[2048,256]{1,0:T(8,128)(2,1)} %x_ref.1, bf16[256,2048]{1,0:T(8,128)(2,1)} %y_ref.1, f32[32,128]{1,0:T(8,128)} %bitcast.6, f32[32,128]{1,0:T(8,128)} %bitcast.7, s32[16,128]{1,0:T(8,128)} %bitcast.8, s32[16,128]{1,0:T(8,128)} %bitcast.9), custom_call_target="tpu_custom_call" | custom-call | tf_op jit(solution)/shard_map/window/pallas_call | solution.py:365
  83.4 3.4 %copy.10 = bf16[2048,2048]{1,0:T(8,128)(2,1)} copy(bf16[2048,2048]{1,0:T(8,128)(2,1)S(1)} %get-tuple-element.6) | data formatting | bytes 16777216
  86.8 0.6 copy.11
